TPU v7x, 256 devices: a whole 4x4x8 slice. The times are simulated.
256 devices in a mesh: rows: 16 (over z, core), cols: 16 (over y, x).
Axes of the slice: x: 4, y: 4, z: 8, core: 2. Of those that a mesh axis runs over, the one named last changes fastest.
Arguments:
- tensor: float32 [32, 2048, 2048], P(None, 'rows', 'cols'), may hold values from -819200 to 819200
- second_init: float32 [2048, 64], P('cols'), may hold values from -6 to 6
- third_init: float32 [32, 64], replicated, may hold values from -6 to 6
Outputs:
- first: float32 [2048, 64], P('rows')
- second: float32 [2048, 64], P('cols')
- third: float32 [32, 64], replicated
All inputs are finite; a program needn't handle non-finite values.
Results may differ from a plain program's by a relative error of at most 0.0003.
Values sent between devices are 32-bit elements; how exact they have to be, the bound alone decides.
No kernel may reach another device: no remote copies, remote signals or barrier semaphores. Data moves between devices by JAX's collectives and lax.ppermute only.
A program may use at most 64 MiB of HBM per device.

v0:
```python
import jax
import jax.numpy as jnp
from jax import lax
from jax.sharding import PartitionSpec as P

ITERS = 5
EPSILON = 1e-05
HIGHEST = lax.Precision.HIGHEST


def solve_right(rhs_rows, system):
    cholesky_low = jnp.linalg.cholesky(system)
    halfway = lax.linalg.triangular_solve(
        cholesky_low, rhs_rows, left_side=False, lower=True, transpose_a=True
    )
    return lax.linalg.triangular_solve(cholesky_low, halfway, left_side=False, lower=True)


def gram_local(factor):
    return jnp.dot(factor.T, factor, precision=HIGHEST, preferred_element_type=jnp.float32)


def settle(raw_share, total_rows):
    squares = lax.psum(jnp.sum(raw_share * raw_share, axis=0), ("rows", "cols"))
    col_scale = jnp.sqrt(squares / total_rows + EPSILON)
    normed = raw_share / col_scale
    gram_whole = lax.psum(gram_local(normed), ("rows", "cols"))
    return (col_scale, gram_whole)


def per_device(tensor, second_init, third_init):
    rows_here = tensor.shape[1]
    cols_here = tensor.shape[2]
    total_first = rows_here * lax.axis_size("rows")
    total_second = cols_here * lax.axis_size("cols")
    share_first = rows_here // lax.axis_size("cols")
    share_second = cols_here // lax.axis_size("rows")
    start_first = lax.axis_index("cols") * share_first
    start_second = lax.axis_index("rows") * share_second
    col_scale, gram_second = settle(
        lax.dynamic_slice_in_dim(second_init, start_second, share_second, 0), total_second
    )
    second = second_init / col_scale
    third = third_init
    gram_third = gram_local(third)
    first = None
    for sweep_index in range(ITERS):
        contract_first = lax.dot_general(
            second,
            tensor,
            (((0,), (2,)), ((), ())),
            precision=HIGHEST,
            preferred_element_type=jnp.float32,
        )
        system_first = gram_third * gram_second
        gram_first = None
        partial_first = jnp.einsum("rki,kr->ir", contract_first, third, precision=HIGHEST)
        mttkrp_first = lax.psum(partial_first, "cols")
        raw_block = solve_right(mttkrp_first, system_first)
        col_scale, gram_first = settle(
            lax.dynamic_slice_in_dim(raw_block, start_first, share_first, 0), total_first
        )
        carried_first = raw_block / col_scale
        contract_second = lax.dot_general(
            carried_first,
            tensor,
            (((0,), (1,)), ((), ())),
            precision=HIGHEST,
            preferred_element_type=jnp.float32,
        )
        partial_second = jnp.einsum("rkj,kr->jr", contract_second, third, precision=HIGHEST)
        outgoing = partial_second
        summed_second = lax.psum(outgoing, "rows")
        first = carried_first
        system_second = gram_third * gram_first
        raw_block = solve_right(summed_second, system_second)
        raw_part = lax.dynamic_slice_in_dim(raw_block, start_second, share_second, 0)
        col_scale, gram_second = settle(raw_part, total_second)
        carried_second = raw_block / col_scale
        partial_third = jnp.einsum("rkj,jr->kr", contract_second, carried_second, precision=HIGHEST)
        outgoing = partial_third
        summed_third = lax.psum(outgoing, ("rows", "cols"))
        second = carried_second
        third = solve_right(summed_third, gram_first * gram_second)
        gram_third = gram_local(third)
    return (first, second, third)


def solution(mesh):
    return jax.shard_map(
        per_device,
        mesh=mesh,
        in_specs=(P(None, "rows", "cols"), P("cols", None), P()),
        out_specs=(P("rows", None), P("cols", None), P()),
        check_vma=False,
    )
```

profile of v0, /device:TPU:1, one launch (start us, length us, event | category | flops | bytes accessed | tf_op | source)
XLA Modules:
  0.0 2455.2 jit_solution(10629154190226435686)
XLA Ops:
  1.7 81.4 %psum.259 = f32[64]{0:T(128)S(1)} all-reduce(f32[64]{0:T(128)S(1)} %multiply_reduce_fusion.10), channel_id=1, replica_groups=mesh['rows'=16,'cols'=16] {'rows','cols'}, use_global_device_ids=true, to_apply=%region_1.0 | all-reduce | flops 64 | bytes 512 | tf_op jit(solution)/shard_map/psum | solution.py:24
  85.1 72.8 %psum.260 = f32[64,64]{0,1:T(8,128)S(1)} all-reduce(f32[64,64]{0,1:T(8,128)S(1)} %fusion.163), channel_id=1, replica_groups=mesh['rows'=16,'cols'=16] {'rows','cols'}, use_global_device_ids=true, to_apply=%region_2.0 | all-reduce | flops 4096 | bytes 32768 | tf_op jit(solution)/shard_map/psum | solution.py:27
  175.8 56.8 %psum.261 = f32[128,64]{0,1:T(8,128)S(1)} all-reduce(f32[128,64]{0,1:T(8,128)S(1)} %bitcast.449), channel_id=1, replica_groups=mesh['rows'=16,'cols'=16] {'cols'}, use_global_device_ids=true, to_apply=%region_5.0 | all-reduce | flops 8192 | bytes 65536 | tf_op jit(solution)/shard_map/psum | solution.py:58
  233.2 86.1 %psum.262 = f32[64]{0:T(128)S(1)} all-reduce(f32[64]{0:T(128)S(1)} %multiply_reduce_fusion.9), channel_id=1, replica_groups=mesh['rows'=16,'cols'=16] {'rows','cols'}, use_global_device_ids=true, to_apply=%region_7.11 | all-reduce | flops 64 | bytes 512 | tf_op jit(solution)/shard_map/psum | solution.py:24
  319.6 73.9 %psum.263 = f32[64,64]{0,1:T(8,128)S(1)} all-reduce(f32[64,64]{0,1:T(8,128)S(1)} %fusion.160), channel_id=1, replica_groups=mesh['rows'=16,'cols'=16] {'rows','cols'}, use_global_device_ids=true, to_apply=%region_8.12 | all-reduce | flops 4096 | bytes 32768 | tf_op jit(solution)/shard_map/psum | solution.py:27
  408.5 44.1 %psum.264 = f32[128,64]{0,1:T(8,128)S(1)} all-reduce(f32[128,64]{0,1:T(8,128)S(1)} %bitcast.450), channel_id=1, replica_groups=mesh['rows'=16,'cols'=16] {'rows'}, use_global_device_ids=true, to_apply=%region_9.13 | all-reduce | flops 8192 | bytes 65536 | tf_op jit(solution)/shard_map/psum | solution.py:73
  453.3 76.4 %psum.265 = f32[64]{0:T(128)S(1)} all-reduce(f32[64]{0:T(128)S(1)} %multiply_reduce_fusion.8), channel_id=1, replica_groups=mesh['rows'=16,'cols'=16] {'rows','cols'}, use_global_device_ids=true, to_apply=%region_11.15 | all-reduce | flops 64 | bytes 512 | tf_op jit(solution)/shard_map/psum | solution.py:24
  532.2 74.2 %all-reduce.4 = (f32[32,64]{0,1:T(8,128)S(1)}, f32[64,64]{0,1:T(8,128)S(1)}) all-reduce(f32[32,64]{0,1:T(8,128)S(1)} %bitcast.444, f32[64,64]{0,1:T(8,128)S(1)} %fusion.157), channel_id=1, replica_groups=mesh['rows'=16,'cols'=16] {'rows','cols'}, use_global_device_ids=true, to_apply=%region_13.17 | all-reduce | flops 6144 | bytes 49152 | tf_op jit(solution)/shard_map/psum | solution.py:82
  635.5 56.8 %psum.268 = f32[128,64]{0,1:T(8,128)S(1)} all-reduce(f32[128,64]{0,1:T(8,128)S(1)} %bitcast.451), channel_id=1, replica_groups=mesh['rows'=16,'cols'=16] {'cols'}, use_global_device_ids=true, to_apply=%region_14.20 | all-reduce | flops 8192 | bytes 65536 | tf_op jit(solution)/shard_map/psum | solution.py:58
  692.9 85.3 %psum.269 = f32[64]{0:T(128)S(1)} all-reduce(f32[64]{0:T(128)S(1)} %multiply_reduce_fusion.7), channel_id=1, replica_groups=mesh['rows'=16,'cols'=16] {'rows','cols'}, use_global_device_ids=true, to_apply=%region_16.22 | all-reduce | flops 64 | bytes 512 | tf_op jit(solution)/shard_map/psum | solution.py:24
  778.5 74.9 %psum.270 = f32[64,64]{0,1:T(8,128)S(1)} all-reduce(f32[64,64]{0,1:T(8,128)S(1)} %fusion.155), channel_id=1, replica_groups=mesh['rows'=16,'cols'=16] {'rows','cols'}, use_global_device_ids=true, to_apply=%region_17.23 | all-reduce | flops 4096 | bytes 32768 | tf_op jit(solution)/shard_map/psum | solution.py:27
  868.3 43.4 %psum.271 = f32[128,64]{0,1:T(8,128)S(1)} all-reduce(f32[128,64]{0,1:T(8,128)S(1)} %bitcast.452), channel_id=1, replica_groups=mesh['rows'=16,'cols'=16] {'rows'}, use_global_device_ids=true, to_apply=%region_18.24 | all-reduce | flops 8192 | bytes 65536 | tf_op jit(solution)/shard_map/psum | solution.py:73
  912.2 76.4 %psum.272 = f32[64]{0:T(128)S(1)} all-reduce(f32[64]{0:T(128)S(1)} %multiply_reduce_fusion.6), channel_id=1, replica_groups=mesh['rows'=16,'cols'=16] {'rows','cols'}, use_global_device_ids=true, to_apply=%region_20.26 | all-reduce | flops 64 | bytes 512 | tf_op jit(solution)/shard_map/psum | solution.py:24
  991.2 74.1 %all-reduce.3 = (f32[32,64]{0,1:T(8,128)S(1)}, f32[64,64]{0,1:T(8,128)S(1)}) all-reduce(f32[32,64]{0,1:T(8,128)S(1)} %bitcast.445, f32[64,64]{0,1:T(8,128)S(1)} %fusion.152), channel_id=1, replica_groups=mesh['rows'=16,'cols'=16] {'rows','cols'}, use_global_device_ids=true, to_apply=%region_22.28 | all-reduce | flops 6144 | bytes 49152 | tf_op jit(solution)/shard_map/psum | solution.py:82
  1094.4 56.8 %psum.275 = f32[128,64]{0,1:T(8,128)S(1)} all-reduce(f32[128,64]{0,1:T(8,128)S(1)} %bitcast.453), channel_id=1, replica_groups=mesh['rows'=16,'cols'=16] {'cols'}, use_global_device_ids=true, to_apply=%region_23.29 | all-reduce | flops 8192 | bytes 65536 | tf_op jit(solution)/shard_map/psum | solution.py:58
  1151.8 85.3 %psum.276 = f32[64]{0:T(128)S(1)} all-reduce(f32[64]{0:T(128)S(1)} %multiply_reduce_fusion.5), channel_id=1, replica_groups=mesh['rows'=16,'cols'=16] {'rows','cols'}, use_global_device_ids=true, to_apply=%region_25.31 | all-reduce | flops 64 | bytes 512 | tf_op jit(solution)/shard_map/psum | solution.py:24
  1237.3 74.7 %psum.277 = f32[64,64]{0,1:T(8,128)S(1)} all-reduce(f32[64,64]{0,1:T(8,128)S(1)} %fusion.150), channel_id=1, replica_groups=mesh['rows'=16,'cols'=16] {'rows','cols'}, use_global_device_ids=true, to_apply=%region_26.32 | all-reduce | flops 4096 | bytes 32768 | tf_op jit(solution)/shard_map/psum | solution.py:27
  1326.9 43.3 %psum.278 = f32[128,64]{0,1:T(8,128)S(1)} all-reduce(f32[128,64]{0,1:T(8,128)S(1)} %bitcast.454), channel_id=1, replica_groups=mesh['rows'=16,'cols'=16] {'rows'}, use_global_device_ids=true, to_apply=%region_27.33 | all-reduce | flops 8192 | bytes 65536 | tf_op jit(solution)/shard_map/psum | solution.py:73
  1370.9 76.4 %psum.279 = f32[64]{0:T(128)S(1)} all-reduce(f32[64]{0:T(128)S(1)} %multiply_reduce_fusion.4), channel_id=1, replica_groups=mesh['rows'=16,'cols'=16] {'rows','cols'}, use_global_device_ids=true, to_apply=%region_29.35 | all-reduce | flops 64 | bytes 512 | tf_op jit(solution)/shard_map/psum | solution.py:24
  1449.8 74.3 %all-reduce.2 = (f32[32,64]{0,1:T(8,128)S(1)}, f32[64,64]{0,1:T(8,128)S(1)}) all-reduce(f32[32,64]{0,1:T(8,128)S(1)} %bitcast.446, f32[64,64]{0,1:T(8,128)S(1)} %fusion.147), channel_id=1, replica_groups=mesh['rows'=16,'cols'=16] {'rows','cols'}, use_global_device_ids=true, to_apply=%region_31.37 | all-reduce | flops 6144 | bytes 49152 | tf_op jit(solution)/shard_map/psum | solution.py:82
  1553.2 56.8 %psum.282 = f32[128,64]{0,1:T(8,128)S(1)} all-reduce(f32[128,64]{0,1:T(8,128)S(1)} %bitcast.455), channel_id=1, replica_groups=mesh['rows'=16,'cols'=16] {'cols'}, use_global_device_ids=true, to_apply=%region_32.38 | all-reduce | flops 8192 | bytes 65536 | tf_op jit(solution)/shard_map/psum | solution.py:58
  1610.6 85.3 %psum.283 = f32[64]{0:T(128)S(1)} all-reduce(f32[64]{0:T(128)S(1)} %multiply_reduce_fusion.3), channel_id=1, replica_groups=mesh['rows'=16,'cols'=16] {'rows','cols'}, use_global_device_ids=true, to_apply=%region_34.40 | all-reduce | flops 64 | bytes 512 | tf_op jit(solution)/shard_map/psum | solution.py:24
  1696.2 74.6 %psum.284 = f32[64,64]{0,1:T(8,128)S(1)} all-reduce(f32[64,64]{0,1:T(8,128)S(1)} %fusion.145), channel_id=1, replica_groups=mesh['rows'=16,'cols'=16] {'rows','cols'}, use_global_device_ids=true, to_apply=%region_35.41 | all-reduce | flops 4096 | bytes 32768 | tf_op jit(solution)/shard_map/psum | solution.py:27
  1785.8 43.4 %psum.285 = f32[128,64]{0,1:T(8,128)S(1)} all-reduce(f32[128,64]{0,1:T(8,128)S(1)} %bitcast.456), channel_id=1, replica_groups=mesh['rows'=16,'cols'=16] {'rows'}, use_global_device_ids=true, to_apply=%region_36.42 | all-reduce | flops 8192 | bytes 65536 | tf_op jit(solution)/shard_map/psum | solution.py:73
  1829.7 76.4 %psum.286 = f32[64]{0:T(128)S(1)} all-reduce(f32[64]{0:T(128)S(1)} %multiply_reduce_fusion.2), channel_id=1, replica_groups=mesh['rows'=16,'cols'=16] {'rows','cols'}, use_global_device_ids=true, to_apply=%region_38.44 | all-reduce | flops 64 | bytes 512 | tf_op jit(solution)/shard_map/psum | solution.py:24
  1908.7 74.2 %all-reduce.1 = (f32[32,64]{0,1:T(8,128)S(1)}, f32[64,64]{0,1:T(8,128)S(1)}) all-reduce(f32[32,64]{0,1:T(8,128)S(1)} %bitcast.447, f32[64,64]{0,1:T(8,128)S(1)} %fusion.142), channel_id=1, replica_groups=mesh['rows'=16,'cols'=16] {'rows','cols'}, use_global_device_ids=true, to_apply=%region_40.46 | all-reduce | flops 6144 | bytes 49152 | tf_op jit(solution)/shard_map/psum | solution.py:82
  2011.9 56.8 %psum.289 = f32[128,64]{0,1:T(8,128)S(1)} all-reduce(f32[128,64]{0,1:T(8,128)S(1)} %bitcast.457), channel_id=1, replica_groups=mesh['rows'=16,'cols'=16] {'cols'}, use_global_device_ids=true, to_apply=%region_41.47 | all-reduce | flops 8192 | bytes 65536 | tf_op jit(solution)/shard_map/psum | solution.py:58
  2069.3 85.3 %psum.290 = f32[64]{0:T(128)S(1)} all-reduce(f32[64]{0:T(128)S(1)} %multiply_reduce_fusion.1), channel_id=1, replica_groups=mesh['rows'=16,'cols'=16] {'rows','cols'}, use_global_device_ids=true, to_apply=%region_43.49 | all-reduce | flops 64 | bytes 512 | tf_op jit(solution)/shard_map/psum | solution.py:24
  2155.0 74.7 %psum.291 = f32[64,64]{0,1:T(8,128)S(1)} all-reduce(f32[64,64]{0,1:T(8,128)S(1)} %fusion.140), channel_id=1, replica_groups=mesh['rows'=16,'cols'=16] {'rows','cols'}, use_global_device_ids=true, to_apply=%region_44.50 | all-reduce | flops 4096 | bytes 32768 | tf_op jit(solution)/shard_map/psum | solution.py:27
  2244.6 43.4 %psum.292 = f32[128,64]{0,1:T(8,128)S(1)} all-reduce(f32[128,64]{0,1:T(8,128)S(1)} %bitcast.458), channel_id=1, replica_groups=mesh['rows'=16,'cols'=16] {'rows'}, use_global_device_ids=true, to_apply=%region_45.51 | all-reduce | flops 8192 | bytes 65536 | tf_op jit(solution)/shard_map/psum | solution.py:73
  2288.5 76.4 %psum.293 = f32[64]{0:T(128)S(1)} all-reduce(f32[64]{0:T(128)S(1)} %multiply_reduce_fusion), channel_id=1, replica_groups=mesh['rows'=16,'cols'=16] {'rows','cols'}, use_global_device_ids=true, to_apply=%region_47.53 | all-reduce | flops 64 | bytes 512 | tf_op jit(solution)/shard_map/psum | solution.py:24
  2367.5 73.9 %all-reduce = (f32[32,64]{0,1:T(8,128)S(1)}, f32[64,64]{0,1:T(8,128)S(1)}) all-reduce(f32[32,64]{0,1:T(8,128)S(1)} %bitcast.448, f32[64,64]{0,1:T(8,128)S(1)} %fusion.138), channel_id=1, replica_groups=mesh['rows'=16,'cols'=16] {'rows','cols'}, use_global_device_ids=true, to_apply=%region_49.55 | all-reduce | flops 6144 | bytes 49152 | tf_op jit(solution)/shard_map/psum | solution.py:82
  (225 shorter events, 244.4 us)
Async XLA Ops:
  0.6 170.5 %copy-start = (f32[32,128,128]{2,1,0:T(8,128)S(1)}, f32[32,128,128]{2,1,0:T(8,128)}, u32[]{:S(2)}) copy-start(f32[32,128,128]{2,1,0:T(8,128)} %param.12) | copy-start | bytes 6291460
  2155.0 89.7 %copy-start.1 = (f32[128,64]{0,1:T(8,128)}, f32[128,64]{0,1:T(8,128)S(1)}, u32[]{:S(2)}) copy-start(f32[128,64]{0,1:T(8,128)S(1)} %broadcast_divide_fusion.1) | copy-start | bytes 98308
  2365.3 89.4 %copy-start.2 = (f32[128,64]{0,1:T(8,128)}, f32[128,64]{0,1:T(8,128)S(1)}, u32[]{:S(2)}) copy-start(f32[128,64]{0,1:T(8,128)S(1)} %broadcast_divide_fusion) | copy-start | bytes 98308
where the time goes:
time: 2470 us; the launch traced here: 2460 us
  blocking collectives  2210 us (89%)
  other arithmetic  185 us (7%)
  matrix products  57.5 us (2%)
    psum x11, blocking collectives, settle(): squares = lax.psum(jnp.sum(raw_share * raw_share, axis=0), ('rows', 'cols'))  891 us
    psum x6, blocking collectives, settle(): gram_whole = lax.psum(gram_local(normed), ('rows', 'cols'))  446 us
    psum x5, blocking collectives, per_device(): summed_third = lax.psum(outgoing, ('rows', 'cols'))  371 us
    psum x5, blocking collectives, per_device(): mttkrp_first = lax.psum(partial_first, 'cols')  284 us
    psum x5, blocking collectives, per_device(): summed_second = lax.psum(outgoing, 'rows')  218 us
    another operation x45, other arithmetic, solve_right(): cholesky_low = jnp.linalg.cholesky(system)  97.8 us
    another operation x30, other arithmetic, solve_right(): lax.linalg.triangular_solve(cholesky_low, halfway, left_side=False, lower...  83.2 us

commit v1 on v0

--- a/solution.py
+++ b/solution.py
@@ -21,7 +21,9 @@
 
 
 def settle(raw_share, total_rows):
-    squares = lax.psum(jnp.sum(raw_share * raw_share, axis=0), ("rows", "cols"))
+    squares = jnp.sum(raw_share * raw_share, axis=0)
+    for mesh_axis in ("cols", "rows"):
+        squares = lax.psum(squares, mesh_axis)
     col_scale = jnp.sqrt(squares / total_rows + EPSILON)
     normed = raw_share / col_scale
     gram_whole = lax.psum(gram_local(normed), ("rows", "cols"))

time: 2470 us -> 2320 us (0.939)
  blocking collectives: 2210 us -> 2060 us
    psum x11 -> x22, blocking collectives: 891 us -> 750 us  [settle(): squares = lax.psum(squares, mesh_axis)]
where the time goes in v1:
time: 2320 us; the launch traced here: 2310 us
  blocking collectives  2060 us (89%)
  other arithmetic  185 us (8%)
  matrix products  57.5 us (2%)
    psum x22, blocking collectives, settle(): squares = lax.psum(squares, mesh_axis)  750 us
    psum x6, blocking collectives, settle(): gram_whole = lax.psum(gram_local(normed), ('rows', 'cols'))  441 us
    psum x5, blocking collectives, per_device(): summed_third = lax.psum(outgoing, ('rows', 'cols'))  366 us
    psum x5, blocking collectives, per_device(): mttkrp_first = lax.psum(partial_first, 'cols')  284 us
    psum x5, blocking collectives, per_device(): summed_second = lax.psum(outgoing, 'rows')  222 us
    another operation x45, other arithmetic, solve_right(): cholesky_low = jnp.linalg.cholesky(system)  97.8 us
    another operation x30, other arithmetic, solve_right(): lax.linalg.triangular_solve(cholesky_low, halfway, left_side=False, lower...  83.2 us

profile of v1, /device:TPU:1, one launch (start us, length us, event | category | flops | bytes accessed | tf_op | source)
XLA Modules:
  0.0 2309.6 jit_solution(9156920346139958190)
XLA Ops:
  1.7 34.3 %psum.336 = f32[64]{0:T(128)S(1)} all-reduce(f32[64]{0:T(128)S(1)} %multiply_reduce_fusion.10), channel_id=1, replica_groups=mesh['rows'=16,'cols'=16] {'cols'}, use_global_device_ids=true, to_apply=%region_1.0 | all-reduce | flops 64 | bytes 512 | tf_op jit(solution)/shard_map/psum | solution.py:26
  36.0 33.8 %psum.337 = f32[64]{0:T(128)S(1)} all-reduce(f32[64]{0:T(128)S(1)} %psum.336), channel_id=1, replica_groups=mesh['rows'=16,'cols'=16] {'rows'}, use_global_device_ids=true, to_apply=%region_2.0 | all-reduce | flops 64 | bytes 512 | tf_op jit(solution)/shard_map/psum | solution.py:26
  71.7 72.8 %psum.338 = f32[64,64]{0,1:T(8,128)S(1)} all-reduce(f32[64,64]{0,1:T(8,128)S(1)} %fusion.163), channel_id=1, replica_groups=mesh['rows'=16,'cols'=16] {'rows','cols'}, use_global_device_ids=true, to_apply=%region_3.0 | all-reduce | flops 4096 | bytes 32768 | tf_op jit(solution)/shard_map/psum | solution.py:29
  162.5 56.7 %psum.339 = f32[128,64]{0,1:T(8,128)S(1)} all-reduce(f32[128,64]{0,1:T(8,128)S(1)} %bitcast.449), channel_id=1, replica_groups=mesh['rows'=16,'cols'=16] {'cols'}, use_global_device_ids=true, to_apply=%region_6.0 | all-reduce | flops 8192 | bytes 65536 | tf_op jit(solution)/shard_map/psum | solution.py:60
  248.2 44.7 %psum.341 = f32[64]{0:T(128)S(1)} all-reduce(f32[64]{0:T(128)S(1)} %psum.340), channel_id=1, replica_groups=mesh['rows'=16,'cols'=16] {'rows'}, use_global_device_ids=true, to_apply=%region_9.13 | all-reduce | flops 64 | bytes 512 | tf_op jit(solution)/shard_map/psum | solution.py:26
  293.3 73.8 %psum.342 = f32[64,64]{0,1:T(8,128)S(1)} all-reduce(f32[64,64]{0,1:T(8,128)S(1)} %fusion.160), channel_id=1, replica_groups=mesh['rows'=16,'cols'=16] {'rows','cols'}, use_global_device_ids=true, to_apply=%region_10.14 | all-reduce | flops 4096 | bytes 32768 | tf_op jit(solution)/shard_map/psum | solution.py:29
  382.1 44.9 %psum.343 = f32[128,64]{0,1:T(8,128)S(1)} all-reduce(f32[128,64]{0,1:T(8,128)S(1)} %bitcast.450), channel_id=1, replica_groups=mesh['rows'=16,'cols'=16] {'rows'}, use_global_device_ids=true, to_apply=%region_11.15 | all-reduce | flops 8192 | bytes 65536 | tf_op jit(solution)/shard_map/psum | solution.py:75
  457.4 33.5 %psum.345 = f32[64]{0:T(128)S(1)} all-reduce(f32[64]{0:T(128)S(1)} %psum.344), channel_id=1, replica_groups=mesh['rows'=16,'cols'=16] {'rows'}, use_global_device_ids=true, to_apply=%region_14.18 | all-reduce | flops 64 | bytes 512 | tf_op jit(solution)/shard_map/psum | solution.py:26
  493.4 73.2 %all-reduce.4 = (f32[32,64]{0,1:T(8,128)S(1)}, f32[64,64]{0,1:T(8,128)S(1)}) all-reduce(f32[32,64]{0,1:T(8,128)S(1)} %bitcast.444, f32[64,64]{0,1:T(8,128)S(1)} %fusion.157), channel_id=1, replica_groups=mesh['rows'=16,'cols'=16] {'rows','cols'}, use_global_device_ids=true, to_apply=%region_16.20 | all-reduce | flops 6144 | bytes 49152 | tf_op jit(solution)/shard_map/psum | solution.py:84
  595.8 56.8 %psum.348 = f32[128,64]{0,1:T(8,128)S(1)} all-reduce(f32[128,64]{0,1:T(8,128)S(1)} %bitcast.451), channel_id=1, replica_groups=mesh['rows'=16,'cols'=16] {'cols'}, use_global_device_ids=true, to_apply=%region_17.23 | all-reduce | flops 8192 | bytes 65536 | tf_op jit(solution)/shard_map/psum | solution.py:60
  681.7 44.6 %psum.350 = f32[64]{0:T(128)S(1)} all-reduce(f32[64]{0:T(128)S(1)} %psum.349), channel_id=1, replica_groups=mesh['rows'=16,'cols'=16] {'rows'}, use_global_device_ids=true, to_apply=%region_20.26 | all-reduce | flops 64 | bytes 512 | tf_op jit(solution)/shard_map/psum | solution.py:26
  726.6 73.5 %psum.351 = f32[64,64]{0,1:T(8,128)S(1)} all-reduce(f32[64,64]{0,1:T(8,128)S(1)} %fusion.155), channel_id=1, replica_groups=mesh['rows'=16,'cols'=16] {'rows','cols'}, use_global_device_ids=true, to_apply=%region_21.27 | all-reduce | flops 4096 | bytes 32768 | tf_op jit(solution)/shard_map/psum | solution.py:29
  815.0 44.3 %psum.352 = f32[128,64]{0,1:T(8,128)S(1)} all-reduce(f32[128,64]{0,1:T(8,128)S(1)} %bitcast.452), channel_id=1, replica_groups=mesh['rows'=16,'cols'=16] {'rows'}, use_global_device_ids=true, to_apply=%region_22.28 | all-reduce | flops 8192 | bytes 65536 | tf_op jit(solution)/shard_map/psum | solution.py:75
  889.6 33.5 %psum.354 = f32[64]{0:T(128)S(1)} all-reduce(f32[64]{0:T(128)S(1)} %psum.353), channel_id=1, replica_groups=mesh['rows'=16,'cols'=16] {'rows'}, use_global_device_ids=true, to_apply=%region_25.31 | all-reduce | flops 64 | bytes 512 | tf_op jit(solution)/shard_map/psum | solution.py:26
  925.7 73.3 %all-reduce.3 = (f32[32,64]{0,1:T(8,128)S(1)}, f32[64,64]{0,1:T(8,128)S(1)}) all-reduce(f32[32,64]{0,1:T(8,128)S(1)} %bitcast.445, f32[64,64]{0,1:T(8,128)S(1)} %fusion.152), channel_id=1, replica_groups=mesh['rows'=16,'cols'=16] {'rows','cols'}, use_global_device_ids=true, to_apply=%region_27.33 | all-reduce | flops 6144 | bytes 49152 | tf_op jit(solution)/shard_map/psum | solution.py:84
  1028.1 56.8 %psum.357 = f32[128,64]{0,1:T(8,128)S(1)} all-reduce(f32[128,64]{0,1:T(8,128)S(1)} %bitcast.453), channel_id=1, replica_groups=mesh['rows'=16,'cols'=16] {'cols'}, use_global_device_ids=true, to_apply=%region_28.34 | all-reduce | flops 8192 | bytes 65536 | tf_op jit(solution)/shard_map/psum | solution.py:60
  1114.0 44.6 %psum.359 = f32[64]{0:T(128)S(1)} all-reduce(f32[64]{0:T(128)S(1)} %psum.358), channel_id=1, replica_groups=mesh['rows'=16,'cols'=16] {'rows'}, use_global_device_ids=true, to_apply=%region_31.37 | all-reduce | flops 64 | bytes 512 | tf_op jit(solution)/shard_map/psum | solution.py:26
  1158.9 73.7 %psum.360 = f32[64,64]{0,1:T(8,128)S(1)} all-reduce(f32[64,64]{0,1:T(8,128)S(1)} %fusion.150), channel_id=1, replica_groups=mesh['rows'=16,'cols'=16] {'rows','cols'}, use_global_device_ids=true, to_apply=%region_32.38 | all-reduce | flops 4096 | bytes 32768 | tf_op jit(solution)/shard_map/psum | solution.py:29
  1247.5 44.3 %psum.361 = f32[128,64]{0,1:T(8,128)S(1)} all-reduce(f32[128,64]{0,1:T(8,128)S(1)} %bitcast.454), channel_id=1, replica_groups=mesh['rows'=16,'cols'=16] {'rows'}, use_global_device_ids=true, to_apply=%region_33.39 | all-reduce | flops 8192 | bytes 65536 | tf_op jit(solution)/shard_map/psum | solution.py:75
  1322.2 33.5 %psum.363 = f32[64]{0:T(128)S(1)} all-reduce(f32[64]{0:T(128)S(1)} %psum.362), channel_id=1, replica_groups=mesh['rows'=16,'cols'=16] {'rows'}, use_global_device_ids=true, to_apply=%region_36.42 | all-reduce | flops 64 | bytes 512 | tf_op jit(solution)/shard_map/psum | solution.py:26
  1358.2 73.2 %all-reduce.2 = (f32[32,64]{0,1:T(8,128)S(1)}, f32[64,64]{0,1:T(8,128)S(1)}) all-reduce(f32[32,64]{0,1:T(8,128)S(1)} %bitcast.446, f32[64,64]{0,1:T(8,128)S(1)} %fusion.147), channel_id=1, replica_groups=mesh['rows'=16,'cols'=16] {'rows','cols'}, use_global_device_ids=true, to_apply=%region_38.44 | all-reduce | flops 6144 | bytes 49152 | tf_op jit(solution)/shard_map/psum | solution.py:84
  1460.6 56.8 %psum.366 = f32[128,64]{0,1:T(8,128)S(1)} all-reduce(f32[128,64]{0,1:T(8,128)S(1)} %bitcast.455), channel_id=1, replica_groups=mesh['rows'=16,'cols'=16] {'cols'}, use_global_device_ids=true, to_apply=%region_39.45 | all-reduce | flops 8192 | bytes 65536 | tf_op jit(solution)/shard_map/psum | solution.py:60
  1546.5 44.6 %psum.368 = f32[64]{0:T(128)S(1)} all-reduce(f32[64]{0:T(128)S(1)} %psum.367), channel_id=1, replica_groups=mesh['rows'=16,'cols'=16] {'rows'}, use_global_device_ids=true, to_apply=%region_42.48 | all-reduce | flops 64 | bytes 512 | tf_op jit(solution)/shard_map/psum | solution.py:26
  1591.4 73.5 %psum.369 = f32[64,64]{0,1:T(8,128)S(1)} all-reduce(f32[64,64]{0,1:T(8,128)S(1)} %fusion.145), channel_id=1, replica_groups=mesh['rows'=16,'cols'=16] {'rows','cols'}, use_global_device_ids=true, to_apply=%region_43.49 | all-reduce | flops 4096 | bytes 32768 | tf_op jit(solution)/shard_map/psum | solution.py:29
  1679.8 44.3 %psum.370 = f32[128,64]{0,1:T(8,128)S(1)} all-reduce(f32[128,64]{0,1:T(8,128)S(1)} %bitcast.456), channel_id=1, replica_groups=mesh['rows'=16,'cols'=16] {'rows'}, use_global_device_ids=true, to_apply=%region_44.50 | all-reduce | flops 8192 | bytes 65536 | tf_op jit(solution)/shard_map/psum | solution.py:75
  1754.4 33.5 %psum.372 = f32[64]{0:T(128)S(1)} all-reduce(f32[64]{0:T(128)S(1)} %psum.371), channel_id=1, replica_groups=mesh['rows'=16,'cols'=16] {'rows'}, use_global_device_ids=true, to_apply=%region_47.53 | all-reduce | flops 64 | bytes 512 | tf_op jit(solution)/shard_map/psum | solution.py:26
  1790.5 73.5 %all-reduce.1 = (f32[32,64]{0,1:T(8,128)S(1)}, f32[64,64]{0,1:T(8,128)S(1)}) all-reduce(f32[32,64]{0,1:T(8,128)S(1)} %bitcast.447, f32[64,64]{0,1:T(8,128)S(1)} %fusion.142), channel_id=1, replica_groups=mesh['rows'=16,'cols'=16] {'rows','cols'}, use_global_device_ids=true, to_apply=%region_49.55 | all-reduce | flops 6144 | bytes 49152 | tf_op jit(solution)/shard_map/psum | solution.py:84
  1893.0 56.8 %psum.375 = f32[128,64]{0,1:T(8,128)S(1)} all-reduce(f32[128,64]{0,1:T(8,128)S(1)} %bitcast.457), channel_id=1, replica_groups=mesh['rows'=16,'cols'=16] {'cols'}, use_global_device_ids=true, to_apply=%region_50.56 | all-reduce | flops 8192 | bytes 65536 | tf_op jit(solution)/shard_map/psum | solution.py:60
  1979.0 44.6 %psum.377 = f32[64]{0:T(128)S(1)} all-reduce(f32[64]{0:T(128)S(1)} %psum.376), channel_id=1, replica_groups=mesh['rows'=16,'cols'=16] {'rows'}, use_global_device_ids=true, to_apply=%region_53.59 | all-reduce | flops 64 | bytes 512 | tf_op jit(solution)/shard_map/psum | solution.py:26
  2024.0 73.4 %psum.378 = f32[64,64]{0,1:T(8,128)S(1)} all-reduce(f32[64,64]{0,1:T(8,128)S(1)} %fusion.140), channel_id=1, replica_groups=mesh['rows'=16,'cols'=16] {'rows','cols'}, use_global_device_ids=true, to_apply=%region_54.60 | all-reduce | flops 4096 | bytes 32768 | tf_op jit(solution)/shard_map/psum | solution.py:29
  2112.3 44.2 %psum.379 = f32[128,64]{0,1:T(8,128)S(1)} all-reduce(f32[128,64]{0,1:T(8,128)S(1)} %bitcast.458), channel_id=1, replica_groups=mesh['rows'=16,'cols'=16] {'rows'}, use_global_device_ids=true, to_apply=%region_55.61 | all-reduce | flops 8192 | bytes 65536 | tf_op jit(solution)/shard_map/psum | solution.py:75
  2223.0 73.1 %all-reduce = (f32[32,64]{0,1:T(8,128)S(1)}, f32[64,64]{0,1:T(8,128)S(1)}) all-reduce(f32[32,64]{0,1:T(8,128)S(1)} %bitcast.448, f32[64,64]{0,1:T(8,128)S(1)} %fusion.138), channel_id=1, replica_groups=mesh['rows'=16,'cols'=16] {'rows','cols'}, use_global_device_ids=true, to_apply=%region_60.66 | all-reduce | flops 6144 | bytes 49152 | tf_op jit(solution)/shard_map/psum | solution.py:84
  (236 shorter events, 569.8 us)
Async XLA Ops:
  0.6 157.1 %copy-start = (f32[32,128,128]{2,1,0:T(8,128)S(1)}, f32[32,128,128]{2,1,0:T(8,128)}, u32[]{:S(2)}) copy-start(f32[32,128,128]{2,1,0:T(8,128)} %param.12) | copy-start | bytes 6291460
  2023.9 88.4 %copy-start.1 = (f32[128,64]{0,1:T(8,128)}, f32[128,64]{0,1:T(8,128)S(1)}, u32[]{:S(2)}) copy-start(f32[128,64]{0,1:T(8,128)S(1)} %broadcast_divide_fusion.1) | copy-start | bytes 98308
  2220.8 88.5 %copy-start.2 = (f32[128,64]{0,1:T(8,128)}, f32[128,64]{0,1:T(8,128)S(1)}, u32[]{:S(2)}) copy-start(f32[128,64]{0,1:T(8,128)S(1)} %broadcast_divide_fusion) | copy-start | bytes 98308
